TPU v7x, 32 devices: a whole 2x2x4 slice. The times are simulated.
32 devices in a mesh: group: 2 (over x), seq: 8 (over z, y), res: 2 (over core).
Axes of the slice: x: 2, y: 2, z: 4, core: 2. Of those that a mesh axis runs over, the one named last changes fastest.
Arguments:
- alignment: bfloat16 [1024, 128, 256], P(('group', 'seq'), 'res'), parts along dimension 0, may hold values from -8 to 8
- ln_gain: float32 [256], replicated, may hold values from 0.5 to 1.5
- ln_bias: float32 [256], replicated, may hold values from -0.6 to 0.6
- w_left: bfloat16 [256, 32], replicated, may hold values from -0.375 to 0.375
- bias_left: float32 [32], replicated, may hold values from -0.6 to 0.6
- w_right: bfloat16 [256, 32], replicated, may hold values from -0.375 to 0.375
- bias_right: float32 [32], replicated, may hold values from -0.6 to 0.6
- w_out: bfloat16 [1024, 128], replicated, may hold values from -1.5 to 1.5
- bias_out: float32 [128], replicated, may hold values from -0.5 to 0.5
Outputs:
- pair_update: bfloat16 [256, 128, 128], P(('group', 'seq'), 'res'), parts along dimension 0
There are 2 independent parts, one for each index of `group`. A program takes and returns all parts, laid end to end along the dimension named above; an argument that names none is the same for every part. Nothing has to cross between parts.
All inputs are finite; a program needn't handle non-finite values.
Results may differ from a plain program's by a relative error of at most 0.0034.
Values may be sent and summed in bfloat16 or wider, within the bound.
No kernel may reach another device: no remote copies, remote signals or barrier semaphores. Data moves between devices by JAX's collectives and lax.ppermute only.
A program may use at most 64 MiB of HBM per device.

v0:
```python
import math

import jax
import jax.numpy as jnp
from jax import lax
from jax.sharding import PartitionSpec as P


def normalize(alignment, ln_gain, ln_bias):
    values = alignment.astype(jnp.float32)
    center = jnp.mean(values, axis=-1, keepdims=True)
    spread = jnp.mean(jnp.square(values - center), axis=-1, keepdims=True)
    return ((values - center) * lax.rsqrt(spread + 1e-05) * ln_gain + ln_bias).astype(jnp.bfloat16)


def project(normed, weight, offset):
    flattened = normed.reshape(-1, normed.shape[-1])
    return (jnp.dot(flattened, weight, preferred_element_type=jnp.float32) + offset).astype(
        jnp.bfloat16
    )


def pair_tile(left_rows, right_rows, weight_cube, rows_here):
    sequences = left_rows.shape[0]
    proj_width = weight_cube.shape[0]
    height = math.gcd(rows_here, 16)
    left_blocks = left_rows.reshape(sequences, rows_here // height, height, proj_width).transpose(
        1, 0, 2, 3
    )
    right_cube = right_rows.reshape(sequences, -1, proj_width)

    def one_block(left_block):
        outers = jnp.einsum(
            "sic,sje->icej", left_block, right_cube, preferred_element_type=jnp.float32
        ).astype(jnp.bfloat16)
        return jnp.einsum("icej,ceo->ijo", outers, weight_cube, preferred_element_type=jnp.float32)

    pieces = lax.map(one_block, left_blocks)
    return pieces.reshape(rows_here, right_cube.shape[1], weight_cube.shape[2])


def shards(alignment, ln_gain, ln_bias, w_left, bias_left, w_right, bias_right, w_out, bias_out):
    sequences = alignment.shape[0]
    residues = alignment.shape[1]
    proj_width = w_left.shape[1]
    out_width = w_out.shape[1]
    normed = normalize(alignment, ln_gain, ln_bias)
    left_rows = project(normed, w_left, bias_left).reshape(sequences, residues * proj_width)
    right_rows = project(normed, w_right, bias_right).reshape(sequences, residues * proj_width)
    weight_cube = w_out.reshape(proj_width, proj_width, out_width)
    columns = lax.all_gather(left_rows, "res", axis=1, tiled=True)
    width_all = columns.shape[1] // proj_width
    devices_seq = lax.axis_size("seq")
    kept_rows = width_all // devices_seq
    summed = lax.psum_scatter(
        pair_tile(columns, right_rows, weight_cube, lax.axis_size("seq") * kept_rows),
        "seq",
        scatter_dimension=0,
        tiled=True,
    )
    return (summed / (sequences * devices_seq) + bias_out).astype(jnp.bfloat16)


def solution(mesh):
    return jax.shard_map(
        shards,
        mesh=mesh,
        in_specs=(P(("group", "seq"), "res", None), P(), P(), P(), P(), P(), P(), P(), P()),
        out_specs=P(("group", "seq"), "res", None),
        check_vma=False,
    )
```

profile of v0, /device:TPU:0, one launch (start us, length us, event | category | flops | bytes accessed | tf_op | source)
XLA Modules:
  0.0 161.4 jit_solution(2791154676896824042)
XLA Ops:
  6.6 2.3 %convert_reduce_fusion = f32[64,64]{1,0:T(8,128)S(1)} fusion(bf16[64,64,256]{2,1,0:T(8,128)(2,1)} %param.11), kind=kLoop, calls=%fused_computation.10 | loop fusion | flops 2093056 | bytes 2113536 | tf_op jit(solution)/shard_map/reduce_sum | solution.py:11
  9.0 2.5 %fusion.16 = f32[64,64]{1,0:T(8,128)S(1)} fusion(bf16[64,64,256]{2,1,0:T(8,128)(2,1)} %param.11, f32[64,64]{1,0:T(8,128)S(1)} %broadcast_multiply_fusion), kind=kLoop, calls=%fused_computation.17 | loop fusion | flops 4190208 | bytes 2129920 | tf_op jit(solution)/shard_map/reduce_sum | solution.py:12
  11.6 1.5 fusion.19
  13.1 1.3 copy-done.2
  16.7 2.4 %all_gather.3 = bf16[64,4096]{1,0:T(8,128)(2,1)} all-gather(bf16[64,2048]{1,0:T(8,128)(2,1)S(1)} %reshape.34), channel_id=1, replica_groups=mesh['group'=2,'seq'=8,'res'=2] {'res'}, dimensions={1}, use_global_device_ids=true | all-gather | bytes 786432 | tf_op jit(solution)/shard_map/all_gather | solution.py:51
  19.1 1.5 copy.12
  21.9 39.8 %while.10 = (s32[]{:T(128)}, f32[8,16,64,128]{3,2,1,0:T(8,128)}, bf16[8,64,16,32]{1,3,2,0:T(8,128)(2,1)S(1)}, bf16[64,64,32]{2,1,0:T(8,128)(2,1)S(1)}, bf16[32,32,128]{2,1,0:T(8,128)(2,1)}, /*index=5*/s32[]{:T(128)}) while((s32[]{:T(128)}, f32[8,16,64,128]{3,2,1,0:T(8,128)}, bf16[8,64,16,32]{1,3,2,0:T(8,128)(2,1)S(1)}, ...), condition=%wide.region_3.4_spmd, body=%wide.region_2.3_spmd.sunk | while | flops 402653184 | bytes 7144037 | solution.py:38
  24.5 2.4 %fusion.36 = f32[8,16,64,128]{3,2,1,0:T(8,128)} fusion(f32[8,16,64,128]{3,2,1,0:T(8,128)} %get-tuple-element.91, s32[]{:T(128)} %get-tuple-element.90, bf16[16,32,64,32]{2,1,3,0:T(8,128)(2,1)S(1)} %fusion.35, bf16[32,32,128]{2,1,0:T(8,128)(2,1)S(1)} %copy-done.10), kind=kOutput, calls=%fused_computation.4.clone.1 | convolution fusion | flops 268435456 | bytes 2884096 | tf_op jit(solution)/shard_map/while/body/eval_jaxpr/icej,ceo->ijo/dot_general | solution.py:36
  28.1 1.3 fusion.35
  29.4 2.4 %fusion.36 = f32[8,16,64,128]{3,2,1,0:T(8,128)} fusion(f32[8,16,64,128]{3,2,1,0:T(8,128)} %get-tuple-element.91, s32[]{:T(128)} %get-tuple-element.90, bf16[16,32,64,32]{2,1,3,0:T(8,128)(2,1)S(1)} %fusion.35, bf16[32,32,128]{2,1,0:T(8,128)(2,1)S(1)} %copy-done.10), kind=kOutput, calls=%fused_computation.4.clone.1 | convolution fusion | flops 268435456 | bytes 2884096 | tf_op jit(solution)/shard_map/while/body/eval_jaxpr/icej,ceo->ijo/dot_general | solution.py:36
  33.1 1.3 fusion.35
  34.4 2.4 %fusion.36 = f32[8,16,64,128]{3,2,1,0:T(8,128)} fusion(f32[8,16,64,128]{3,2,1,0:T(8,128)} %get-tuple-element.91, s32[]{:T(128)} %get-tuple-element.90, bf16[16,32,64,32]{2,1,3,0:T(8,128)(2,1)S(1)} %fusion.35, bf16[32,32,128]{2,1,0:T(8,128)(2,1)S(1)} %copy-done.10), kind=kOutput, calls=%fused_computation.4.clone.1 | convolution fusion | flops 268435456 | bytes 2884096 | tf_op jit(solution)/shard_map/while/body/eval_jaxpr/icej,ceo->ijo/dot_general | solution.py:36
  38.1 1.3 fusion.35
  39.3 2.4 %fusion.36 = f32[8,16,64,128]{3,2,1,0:T(8,128)} fusion(f32[8,16,64,128]{3,2,1,0:T(8,128)} %get-tuple-element.91, s32[]{:T(128)} %get-tuple-element.90, bf16[16,32,64,32]{2,1,3,0:T(8,128)(2,1)S(1)} %fusion.35, bf16[32,32,128]{2,1,0:T(8,128)(2,1)S(1)} %copy-done.10), kind=kOutput, calls=%fused_computation.4.clone.1 | convolution fusion | flops 268435456 | bytes 2884096 | tf_op jit(solution)/shard_map/while/body/eval_jaxpr/icej,ceo->ijo/dot_general | solution.py:36
  43.0 1.3 fusion.35
  44.3 2.4 %fusion.36 = f32[8,16,64,128]{3,2,1,0:T(8,128)} fusion(f32[8,16,64,128]{3,2,1,0:T(8,128)} %get-tuple-element.91, s32[]{:T(128)} %get-tuple-element.90, bf16[16,32,64,32]{2,1,3,0:T(8,128)(2,1)S(1)} %fusion.35, bf16[32,32,128]{2,1,0:T(8,128)(2,1)S(1)} %copy-done.10), kind=kOutput, calls=%fused_computation.4.clone.1 | convolution fusion | flops 268435456 | bytes 2884096 | tf_op jit(solution)/shard_map/while/body/eval_jaxpr/icej,ceo->ijo/dot_general | solution.py:36
  48.0 1.3 fusion.35
  49.3 2.4 %fusion.36 = f32[8,16,64,128]{3,2,1,0:T(8,128)} fusion(f32[8,16,64,128]{3,2,1,0:T(8,128)} %get-tuple-element.91, s32[]{:T(128)} %get-tuple-element.90, bf16[16,32,64,32]{2,1,3,0:T(8,128)(2,1)S(1)} %fusion.35, bf16[32,32,128]{2,1,0:T(8,128)(2,1)S(1)} %copy-done.10), kind=kOutput, calls=%fused_computation.4.clone.1 | convolution fusion | flops 268435456 | bytes 2884096 | tf_op jit(solution)/shard_map/while/body/eval_jaxpr/icej,ceo->ijo/dot_general | solution.py:36
  53.0 1.3 fusion.35
  54.3 2.4 %fusion.36 = f32[8,16,64,128]{3,2,1,0:T(8,128)} fusion(f32[8,16,64,128]{3,2,1,0:T(8,128)} %get-tuple-element.91, s32[]{:T(128)} %get-tuple-element.90, bf16[16,32,64,32]{2,1,3,0:T(8,128)(2,1)S(1)} %fusion.35, bf16[32,32,128]{2,1,0:T(8,128)(2,1)S(1)} %copy-done.10), kind=kOutput, calls=%fused_computation.4.clone.1 | convolution fusion | flops 268435456 | bytes 2884096 | tf_op jit(solution)/shard_map/while/body/eval_jaxpr/icej,ceo->ijo/dot_general | solution.py:36
  57.9 1.3 fusion.35
  59.2 2.4 %fusion.36 = f32[8,16,64,128]{3,2,1,0:T(8,128)} fusion(f32[8,16,64,128]{3,2,1,0:T(8,128)} %get-tuple-element.91, s32[]{:T(128)} %get-tuple-element.90, bf16[16,32,64,32]{2,1,3,0:T(8,128)(2,1)S(1)} %fusion.35, bf16[32,32,128]{2,1,0:T(8,128)(2,1)S(1)} %copy-done.10), kind=kOutput, calls=%fused_computation.4.clone.1 | convolution fusion | flops 268435456 | bytes 2884096 | tf_op jit(solution)/shard_map/while/body/eval_jaxpr/icej,ceo->ijo/dot_general | solution.py:36
  61.7 91.1 %reduce-scatter.2.cloned.1.call-done = f32[16,64,128]{2,1,0:T(8,128)} async-done(((f32[128,64,128]{2,1,0:T(8,128)}), f32[16,64,128]{2,1,0:T(8,128)}) %reduce-scatter.2.cloned.1.call-update) | async-done | bytes 524304 | tf_op jit(solution)/shard_map/reduce_scatter | solution.py:55
  152.8 1.8 %add_convert_fusion = bf16[16,64,128]{2,1,0:T(8,128)(2,1)} fusion(f32[16,64,128]{2,1,0:T(8,128)} %reduce-scatter.2.cloned.1.call-done, f32[128]{0:T(128)S(1)} %copy-done.7), kind=kLoop, calls=%fused_computation.21 | loop fusion | flops 393216 | bytes 786944 | tf_op jit(solution)/shard_map/convert_element_type | solution.py:61
  (70 shorter events, 14.7 us)
Async XLA Ops:
  6.5 7.8 %copy-start = (bf16[256,32]{0,1:T(8,128)(2,1)S(1)}, bf16[256,32]{0,1:T(8,128)(2,1)}, u32[]{:S(2)}) copy-start(bf16[256,32]{0,1:T(8,128)(2,1)} %param.14) | copy-start | bytes 49156
  6.5 5.0 %copy-start.1 = (bf16[64,64,256]{2,1,0:T(8,128)(2,1)S(1)}, bf16[64,64,256]{2,1,0:T(8,128)(2,1)}, u32[]{:S(2)}) copy-start(bf16[64,64,256]{2,1,0:T(8,128)(2,1)} %param.11) | copy-start | bytes 6291460
  6.5 5.0 %copy-start.6 = (f32[256]{0:T(256)S(1)}, f32[256]{0:T(256)}, u32[]{:S(2)}) copy-start(f32[256]{0:T(256)} %param.12) | copy-start | bytes 3076
  6.5 5.0 %copy-start.5 = (f32[256]{0:T(256)S(1)}, f32[256]{0:T(256)}, u32[]{:S(2)}) copy-start(f32[256]{0:T(256)} %param.13) | copy-start | bytes 3076
  6.5 146.2 %reduce-scatter.2.cloned.1.call-start = ((), (), s32[]{:S(2)}) async-start(), calls=%async_computation.1 | async-start | bytes 4718592 | tf_op jit(solution)/shard_map/reduce_scatter | solution.py:55
  6.6 7.8 %copy-start.8 = (f32[32]{0:T(128)S(1)}, f32[32]{0:T(128)}, u32[]{:S(2)}) copy-start(f32[32]{0:T(128)} %param.15) | copy-start | bytes 388
  13.0 1.3 copy-start.2
  13.0 7.6 %copy-start.4 = (bf16[256,32]{0,1:T(8,128)(2,1)S(1)}, bf16[256,32]{0,1:T(8,128)(2,1)}, u32[]{:S(2)}) copy-start(bf16[256,32]{0,1:T(8,128)(2,1)} %param.16) | copy-start | bytes 49156
  13.1 7.6 %copy-start.9 = (f32[32]{0:T(128)S(1)}, f32[32]{0:T(128)}, u32[]{:S(2)}) copy-start(f32[32]{0:T(128)} %param.17) | copy-start | bytes 388
  15.1 5.6 %copy-start.3 = (bf16[64,64,256]{2,1,0:T(8,128)(2,1)S(1)}, bf16[64,64,256]{2,1,0:T(8,128)(2,1)}, u32[]{:S(2)}) copy-start(bf16[64,64,256]{2,1,0:T(8,128)(2,1)} %copy-done.2) | copy-start | bytes 6291460
  21.9 2.5 %copy-start.10 = (bf16[32,32,128]{2,1,0:T(8,128)(2,1)S(1)}, bf16[32,32,128]{2,1,0:T(8,128)(2,1)}, u32[]{:S(2)}) copy-start(bf16[32,32,128]{2,1,0:T(8,128)(2,1)} %get-tuple-element.100) | copy-start | bytes 786436 | tf_op jit(solution)/shard_map/while
  26.9 2.5 %copy-start.10 = (bf16[32,32,128]{2,1,0:T(8,128)(2,1)S(1)}, bf16[32,32,128]{2,1,0:T(8,128)(2,1)}, u32[]{:S(2)}) copy-start(bf16[32,32,128]{2,1,0:T(8,128)(2,1)} %get-tuple-element.100) | copy-start | bytes 786436 | tf_op jit(solution)/shard_map/while
  31.9 2.5 %copy-start.10 = (bf16[32,32,128]{2,1,0:T(8,128)(2,1)S(1)}, bf16[32,32,128]{2,1,0:T(8,128)(2,1)}, u32[]{:S(2)}) copy-start(bf16[32,32,128]{2,1,0:T(8,128)(2,1)} %get-tuple-element.100) | copy-start | bytes 786436 | tf_op jit(solution)/shard_map/while
  36.8 2.5 %copy-start.10 = (bf16[32,32,128]{2,1,0:T(8,128)(2,1)S(1)}, bf16[32,32,128]{2,1,0:T(8,128)(2,1)}, u32[]{:S(2)}) copy-start(bf16[32,32,128]{2,1,0:T(8,128)(2,1)} %get-tuple-element.100) | copy-start | bytes 786436 | tf_op jit(solution)/shard_map/while
  41.8 2.5 %copy-start.10 = (bf16[32,32,128]{2,1,0:T(8,128)(2,1)S(1)}, bf16[32,32,128]{2,1,0:T(8,128)(2,1)}, u32[]{:S(2)}) copy-start(bf16[32,32,128]{2,1,0:T(8,128)(2,1)} %get-tuple-element.100) | copy-start | bytes 786436 | tf_op jit(solution)/shard_map/while
  46.8 2.5 %copy-start.10 = (bf16[32,32,128]{2,1,0:T(8,128)(2,1)S(1)}, bf16[32,32,128]{2,1,0:T(8,128)(2,1)}, u32[]{:S(2)}) copy-start(bf16[32,32,128]{2,1,0:T(8,128)(2,1)} %get-tuple-element.100) | copy-start | bytes 786436 | tf_op jit(solution)/shard_map/while
  51.7 2.5 %copy-start.10 = (bf16[32,32,128]{2,1,0:T(8,128)(2,1)S(1)}, bf16[32,32,128]{2,1,0:T(8,128)(2,1)}, u32[]{:S(2)}) copy-start(bf16[32,32,128]{2,1,0:T(8,128)(2,1)} %get-tuple-element.100) | copy-start | bytes 786436 | tf_op jit(solution)/shard_map/while
  56.7 2.5 %copy-start.10 = (bf16[32,32,128]{2,1,0:T(8,128)(2,1)S(1)}, bf16[32,32,128]{2,1,0:T(8,128)(2,1)}, u32[]{:S(2)}) copy-start(bf16[32,32,128]{2,1,0:T(8,128)(2,1)} %get-tuple-element.100) | copy-start | bytes 786436 | tf_op jit(solution)/shard_map/while
  61.7 91.1 %copy-start.7 = (f32[128]{0:T(128)S(1)}, f32[128]{0:T(128)}, u32[]{:S(2)}) copy-start(f32[128]{0:T(128)} %param.19) | copy-start | bytes 1540
Sparse Core Ops, SparseCore 0:
  61.8 90.9 reduce-scatter.1
where the time goes:
time: 162 us; the launch traced here: 161 us
  waiting for transfers between devices  91.1 us (56%)
  matrix products  31.1 us (19%)
  local copies, waits for them, and re-layouts  14.7 us (9%)
  between operations  13.6 us (8%)
  other arithmetic  8.18 us (5%)
  blocking collectives  2.43 us (2%)
    reduce_scatter x1, waiting for transfers between devices, shards(): lax.psum_scatter(pair_tile(columns, right_rows, weight_cube, lax.axis_siz...  91.1 us
    dot_general x8, matrix products, one_block(): jnp.einsum('icej,ceo->ijo', outers, weight_cube, preferred_element_type=j...  19.5 us
    dot_general x8, matrix products, one_block(): jnp.einsum('sic,sje->icej', left_block, right_cube, preferred_element_typ...  10.2 us
    another operation x8, local copies, waits for them, and re-layouts  7.64 us
  transfers between devices with their start and end apart: 1, of which 1 were waited for; matrix products, arithmetic and copies ran while one was open for 0% of the time, Pallas kernels for 0%

commit v1 on v0

v1 whole, which is shorter than its diff:
```python
import functools

import jax
import jax.numpy as jnp
from jax import lax
from jax.experimental import pallas as pl
from jax.experimental.pallas import tpu as pltpu
from jax.sharding import PartitionSpec as P

LANES = 128
ROWS = 16


def ring_order(count):
    return list(range(0, count, 2)) + [q for q in range(count - 1, -1, -1) if q % 2]


def project_kernel(
    x_ref, gain_ref, bias_ref, wl_ref, wr_ref, bl_ref, br_ref,
    left_ref, right_ref, values, normed, weights,
):
    seqs, residues, channels = x_ref.shape
    width = wl_ref.shape[0]
    fold = LANES // width
    groups = residues // fold

    @pl.when(pl.program_id(0) == 0)
    def _():
        row = lax.broadcasted_iota(jnp.int32, (width, LANES), 0)
        lane = lax.broadcasted_iota(jnp.int32, (width, LANES), 1)
        spread = (lane % width == row).astype(jnp.bfloat16)
        lane_wide = lax.broadcasted_iota(jnp.int32, (channels, LANES), 1)
        for side, w_ref in enumerate((wl_ref, wr_ref)):
            tiled = lax.dot_general(
                w_ref[...], spread, (((0,), (0,)), ((), ())), preferred_element_type=jnp.float32
            )
            for k in range(fold):
                weights[k * channels : (k + 1) * channels, side * LANES : (side + 1) * LANES] = (
                    jnp.where(lane_wide // width == k, tiled, 0.0).astype(jnp.bfloat16)
                )

    parts = channels // LANES
    for p in range(parts):
        values[p] = x_ref[:, :, p * LANES : (p + 1) * LANES].astype(jnp.float32).reshape(
            seqs * residues, LANES
        )
    gain = gain_ref[...]
    bias = bias_ref[...]

    for g in range(groups):
        for k in range(fold):
            v = jnp.concatenate(
                [values[p, pl.ds(g * fold + k, seqs, stride=residues), :] for p in range(parts)],
                axis=1,
            )
            center = jnp.mean(v, axis=-1, keepdims=True)
            d = v - center
            spread2 = jnp.mean(d * d, axis=-1, keepdims=True)
            normed[g * seqs : (g + 1) * seqs, k * channels : (k + 1) * channels] = (
                d * lax.rsqrt(spread2 + 1e-05) * gain + bias
            ).astype(jnp.bfloat16)
    offset = jnp.concatenate([bl_ref[...]] * fold + [br_ref[...]] * fold, axis=1)
    out = (
        jnp.dot(normed[...], weights[...], preferred_element_type=jnp.float32) + offset
    ).astype(jnp.bfloat16)
    for g in range(groups):
        rows = out[g * seqs : (g + 1) * seqs]
        left_ref[:, g * LANES : (g + 1) * LANES] = rows[:, :LANES]
        right_ref[:, g * LANES : (g + 1) * LANES] = rows[:, LANES:]


def project(alignment, ln_gain, ln_bias, w_left, bias_left, w_right, bias_right):
    seqs, residues, channels = alignment.shape
    width = w_left.shape[1]
    block = ROWS
    whole = lambda shape: pl.BlockSpec(shape, lambda s: (0,) * len(shape))
    wide = residues * width
    fold = LANES // width
    return pl.pallas_call(
        project_kernel,
        grid=(seqs // block,),
        in_specs=[
            pl.BlockSpec((block, residues, channels), lambda s: (s, 0, 0)),
            whole((1, channels)), whole((1, channels)),
            whole((width, channels)), whole((width, channels)),
            whole((1, width)), whole((1, width)),
        ],
        out_specs=[
            pl.BlockSpec((block, wide), lambda s: (s, 0)),
            pl.BlockSpec((block, wide), lambda s: (s, 0)),
        ],
        out_shape=[jax.ShapeDtypeStruct((seqs, wide), jnp.bfloat16)] * 2,
        scratch_shapes=[
            pltpu.VMEM((channels // LANES, block * residues, LANES), jnp.float32),
            pltpu.VMEM((block * residues // fold, fold * channels), jnp.bfloat16),
            pltpu.VMEM((fold * channels, 2 * LANES), jnp.bfloat16),
        ],
        name="project",
    )(
        alignment, ln_gain[None], ln_bias[None], w_left.T, w_right.T,
        bias_left[None], bias_right[None],
    )


def spread_weights(w_out, width):
    fold = LANES // width
    out_width = w_out.shape[1]
    cube = w_out.reshape(width, 1, width, 1, out_width)
    same = jnp.eye(fold, dtype=jnp.bool_)[None, :, None, :, None]
    return jnp.where(same, cube, jnp.zeros((), w_out.dtype)).reshape(
        width * fold * width, fold * out_width
    )


def pair_kernel(count, kept, width, scale, order_ref, left_ref, spread_ref, bias_ref, *refs):
    rights = refs[: count + 1]
    out_ref, lefts, turned, product, result = refs[count + 1 :]
    halves, _, half_rows, left_wide = left_ref.shape
    seqs = halves * half_rows
    wide = rights[0].shape[1]
    fold = LANES // width
    groups = wide // LANES
    out_width = spread_ref.shape[1] // fold
    for d in range(count):
        for h in range(halves):
            start = d * seqs + h * half_rows
            lefts[start : start + half_rows, :] = left_ref[h, order_ref[d]]
    row = lax.broadcasted_iota(jnp.int32, (width * ROWS, left_wide), 0)
    lane = lax.broadcasted_iota(jnp.int32, (width * ROWS, left_wide), 1)
    pick = (lane == (row % ROWS) * width + row // ROWS).astype(jnp.bfloat16)
    turned[...] = lax.dot_general(
        pick, lefts[...], (((1,), (1,)), ((), ())), preferred_element_type=jnp.float32
    ).astype(jnp.bfloat16)
    for g in range(0, groups, 2):
        many = min(2, groups - g)
        columns = jnp.concatenate(
            [r[:, g * LANES : (g + many) * LANES] for r in rights], axis=0
        )
        outer = jnp.dot(turned[...], columns, preferred_element_type=jnp.float32).astype(
            jnp.bfloat16
        )
        for m in range(many):
            for c in range(width):
                product[(g + m) * ROWS : (g + m + 1) * ROWS, c * LANES : (c + 1) * LANES] = outer[
                    c * ROWS : (c + 1) * ROWS, m * LANES : (m + 1) * LANES
                ]
    summed = jnp.dot(product[...], spread_ref[...], preferred_element_type=jnp.float32)
    columns_here = groups * fold
    for g in range(groups):
        for k in range(fold):
            result[pl.ds(g * fold + k, ROWS, stride=columns_here), :] = summed[
                g * ROWS : (g + 1) * ROWS, k * out_width : (k + 1) * out_width
            ]
    for i in range(kept):
        out_ref[i] = (
            result[i * columns_here : (i + 1) * columns_here, :] * scale + bias_ref[...]
        ).astype(jnp.bfloat16)


def pair_update(order, left, spread, bias_out, rights, kept, width, total):
    count = left.shape[1]
    wide = rights[0].shape[1]
    out_width = bias_out.shape[0]
    columns_here = wide // width
    vmem = pl.BlockSpec(memory_space=pltpu.VMEM)
    groups = wide // LANES
    return pl.pallas_call(
        functools.partial(pair_kernel, count, kept, width, 1.0 / total),
        in_specs=[pl.BlockSpec(memory_space=pltpu.SMEM)] + [vmem] * (3 + len(rights)),
        out_specs=vmem,
        out_shape=jax.ShapeDtypeStruct((kept, columns_here, out_width), jnp.bfloat16),
        scratch_shapes=[
            pltpu.VMEM((total, left.shape[3]), jnp.bfloat16),
            pltpu.VMEM((width * ROWS, total), jnp.bfloat16),
            pltpu.VMEM((groups * ROWS, width * LANES), jnp.bfloat16),
            pltpu.VMEM((ROWS * columns_here, out_width), jnp.float32),
        ],
        name="pair",
    )(order, left, spread, bias_out[None], *rights)


def shards(alignment, ln_gain, ln_bias, w_left, bias_left, w_right, bias_right, w_out, bias_out):
    seqs, residues, _ = alignment.shape
    width = w_left.shape[1]
    count = lax.axis_size("seq")
    pair = lax.axis_size("res")
    kept = residues * pair // count
    left, right = project(alignment, ln_gain, ln_bias, w_left, bias_left, w_right, bias_right)
    spread = spread_weights(w_out, width)

    order = ring_order(count)
    ahead = [(order[p], order[(p + 1) % count]) for p in range(count)]
    back = [(b, a) for a, b in ahead]
    place = [order.index(q) for q in range(count)]
    position = jnp.asarray(place, jnp.int32)[lax.axis_index("seq")]

    rights = [right]
    offsets = [0]
    up = down = right
    for d in range(1, count // 2):
        up = lax.ppermute(up, "seq", ahead)
        down = lax.ppermute(down, "seq", back)
        rights += [up, down]
        offsets += [-d, d]
    half = seqs // 2
    rights += [
        lax.ppermute(up[:half], "seq", ahead), lax.ppermute(down[half:], "seq", back)
    ]
    offsets += [count // 2]
    sources = jnp.asarray(order, jnp.int32)[(position + jnp.asarray(offsets, jnp.int32)) % count]

    blocks = left.reshape(pair, seqs // pair, count // pair, kept * width).transpose(0, 2, 1, 3)
    blocks = lax.all_to_all(blocks, "res", 0, 0, tiled=True)
    blocks = blocks.reshape(count, seqs // pair, kept * width)
    blocks = lax.all_to_all(blocks, "seq", 0, 0, tiled=True)
    blocks = lax.all_gather(blocks, "res", axis=0)
    return pair_update(
        sources, blocks, spread, bias_out, rights, kept, width, seqs * count
    )


def solution(mesh):
    return jax.shard_map(
        shards,
        mesh=mesh,
        in_specs=(P(("group", "seq"), "res", None), P(), P(), P(), P(), P(), P(), P(), P()),
        out_specs=P(("group", "seq"), "res", None),
        check_vma=False,
    )
```

time: 162 us -> 56.2 us (0.35)
  waiting for transfers between devices: 91.1 us -> 5.78 us
  matrix products: 31.1 us -> 0 us
  starting transfers between devices: 0.03 us -> 16.7 us
  between operations: 13.6 us -> 0.09 us
  Pallas kernels: 0 us -> 13.4 us
  local copies, waits for them, and re-layouts: 14.7 us -> 9.3 us
  other arithmetic: 8.18 us -> 4.33 us
  blocking collectives: 2.43 us -> 6.25 us
    reduce_scatter x1 -> x0, waiting for transfers between devices: 91.1 us -> none  [shards(): lax.psum_scatter(pair_tile(columns, right_rows, weight_cube, lax.axis_siz...]
    dot_general x18 -> x0, matrix products: 31.1 us -> none  [the longest x8 19.5 us: one_block(): jnp.einsum('icej,ceo->ijo', outers, weight_cube, preferred_element_type=j...]
    pallas_call x0 -> x2, Pallas kernels: none -> 13.4 us  [the longest x1 6.79 us: project(): pl.pallas_call(project_kernel, grid=(seqs // block,), in_specs=[pl.BlockS...]
    ppermute x0 -> x8, starting transfers between devices: none -> 10.5 us  [the longest x3 7.08 us: shards(): up = lax.ppermute(up, 'seq', ahead)]
    another operation x8 -> x0, local copies, waits for them, and re-layouts: 7.64 us -> none
    all_to_all x0 -> x1, starting transfers between devices: none -> 6.28 us  [shards(): blocks = lax.all_to_all(blocks, 'seq', 0, 0, tiled=True)]
    ppermute x0 -> x8, waiting for transfers between devices: none -> 5.78 us  [the longest x3 3.61 us: shards(): up = lax.ppermute(up, 'seq', ahead)]
    reduce_sum x2 -> x0, other arithmetic: 4.87 us -> none  [the longest x1 2.53 us: normalize(): spread = jnp.mean(jnp.square(values - center), axis=-1, keepdims=True)]
  transfers between devices with their start and end apart: 1 -> 9, of which waited for: 1 -> 4; matrix products, arithmetic and copies ran while one was open for 0% -> 23% of each run, Pallas kernels for 0% -> 0%
where the time goes in v1:
time: 56.2 us; the launch traced here: 55.8 us
  starting transfers between devices  16.7 us (30%)
  Pallas kernels  13.4 us (24%)
  local copies, waits for them, and re-layouts  9.3 us (17%)
  blocking collectives  6.25 us (11%)
  waiting for transfers between devices  5.78 us (10%)
  other arithmetic  4.33 us (8%)
    ppermute x3, starting transfers between devices, shards(): up = lax.ppermute(up, 'seq', ahead)  7.08 us
    pallas_call x1, Pallas kernels, project(): pl.pallas_call(project_kernel, grid=(seqs // block,), in_specs=[pl.BlockS...  6.79 us
    pallas_call x1, Pallas kernels, pair_update(): pl.pallas_call(functools.partial(pair_kernel, count, kept, width, 1.0 / t...  6.56 us
    all_to_all x1, starting transfers between devices, shards(): blocks = lax.all_to_all(blocks, 'seq', 0, 0, tiled=True)  6.28 us
    unnamed x25, local copies, waits for them, and re-layouts  5.54 us
    all_to_all x1, blocking collectives, shards(): blocks = lax.all_to_all(blocks, 'res', 0, 0, tiled=True)  3.94 us
    select_n x1, other arithmetic, spread_weights(): jnp.where(same, cube, jnp.zeros((), w_out.dtype))  3.61 us
    ppermute x3, waiting for transfers between devices, shards(): up = lax.ppermute(up, 'seq', ahead)  3.61 us
  transfers between devices with their start and end apart: 9, of which 4 were waited for; matrix products, arithmetic and copies ran while one was open for 23% of the time, Pallas kernels for 0%

profile of v1, /device:TPU:0, one launch (start us, length us, event | category | flops | bytes accessed | tf_op | source)
XLA Modules:
  0.0 55.8 jit_solution(13745205909566072694)
XLA Ops:
  0.0 6.8 %project.1 = (bf16[64,2048]{1,0:T(8,128)(2,1)}, bf16[64,2048]{1,0:T(8,128)(2,1)}) custom-call(bf16[64,64,256]{2,1,0:T(8,128)(2,1)} %x_ref.1, f32[1,256]{1,0:T(1,128)} %bitcast.24, f32[1,256]{1,0:T(1,128)} %bitcast.25, bf16[32,256]{1,0:T(8,128)(2,1)} %bitcast.22, bf16[32,256]{1,0:T(8,128)(2,1)} %bitcast.23, f32[1,32]{1,0:T(1,128)} %bitcast.26, f32[1,32]{1,0:T(1,128)} %bitcast.27), custom_call_target="tpu_custom_call" | custom-call | tf_op jit(solution)/shard_map/project/pallas_call | solution.py:79
  6.8 3.1 %collective-permute-start = (bf16[64,2048]{1,0:T(8,128)(2,1)}, bf16[64,2048]{1,0:T(8,128)(2,1)S(1)}, u32[]{:S(2)}, u32[]{:S(2)}) collective-permute-start(bf16[64,2048]{1,0:T(8,128)(2,1)} %get-tuple-element.8.refs_0_), channel_id=1, source_target_pairs={{0,4},{4,8},{8,12},{12,14},{14,10},{10,6},{6,2},{2,0},{1,5},{5,9},... | collective-permute-start | bytes 786440 | tf_op jit(solution)/shard_map/ppermute | solution.py:201
  9.9 1.1 %reshape.20 = bf16[2,32,4,512]{3,2,1,0:T(4,128)(2,1)S(1)} reshape(bf16[64,2048]{1,0:T(8,128)(2,1)} %get-tuple-element.7) | data formatting | bytes 524288 | tf_op jit(solution)/shard_map/reshape | solution.py:212
  11.0 3.9 %all_to_all.10 = bf16[2,4,32,512]{3,1,2,0:T(4,128)(2,1)S(1)} all-to-all(bf16[2,4,32,512]{3,1,2,0:T(4,128)(2,1)S(1)} %bitcast.20), channel_id=1, replica_groups=mesh['group'=2,'seq'=8,'res'=2] {'res'}, dimensions={0} | all-to-all | bytes 524288 | tf_op jit(solution)/shard_map/all_to_all | solution.py:213
  14.9 0.8 %copy.15 = bf16[2,4,32,512]{3,2,1,0:T(8,128)(2,1)} copy(bf16[2,4,32,512]{3,1,2,0:T(4,128)(2,1)S(1)} %all_to_all.10) | data formatting | bytes 524288 | tf_op jit(solution)/shard_map/all_to_all | solution.py:213
  15.7 6.3 %all-to-all-start.1 = ((bf16[8,32,512]{2,1,0:T(8,128)(2,1)}), bf16[8,32,512]{2,1,0:T(8,128)(2,1)S(1)}, u32[]{:S(2)}, u32[]{:S(2)}) async-start(bf16[8,32,512]{2,1,0:T(8,128)(2,1)} %bitcast.8), calls=%async_computation.1 | async-start | bytes 524288 | tf_op jit(solution)/shard_map/all_to_all | solution.py:215
  22.0 2.1 %collective-permute-start.2 = (bf16[64,2048]{1,0:T(8,128)(2,1)S(1)}, bf16[64,2048]{1,0:T(8,128)(2,1)S(1)}, u32[]{:S(2)}, u32[]{:S(2)}) collective-permute-start(bf16[64,2048]{1,0:T(8,128)(2,1)S(1)} %collective-permute-done.refs_1_), channel_id=1, source_target_pairs={{0,4},{4,8},{8,12},{12,14},{14,10},{10,6},{6,2},{2,0},{1,5},{5,9},... | collective-permute-start | bytes 786440 | tf_op jit(solution)/shard_map/ppermute | solution.py:201
  24.1 0.1 collective-permute-start.3
  24.2 3.6 %broadcast_select_fusion = bf16[32,4,32,4,128]{4,3,2,1,0:T(4,128)(2,1)} fusion(pred[4,4]{1,0:T(4,128)(4,1)S(1)} %iota_compare_fusion, bf16[32,32,128]{2,1,0:T(8,128)(2,1)S(1)} %bitcast.21), kind=kLoop, calls=%fused_computation.2 | loop fusion | flops 2097152 | bytes 4456464 | tf_op jit(solution)/shard_map/jit(_where)/select_n | solution.py:110
  27.8 4.9 %copy.18 = bf16[512,8,4,128]{3,1,2,0:T(8,128)(2,1)} copy(bf16[512,8,4,128]{3,2,1,0:T(4,128)(2,1)} %bitcast.18) | data formatting | bytes 8388608
  32.7 0.7 %dynamic_slice.3 = s32[1]{0:T(128)} dynamic-slice(s32[8]{0:T(128)S(1)} %copy-done.11, s32[]{:T(128)S(6)} %select_n.21), dynamic_slice_sizes={1} | dynamic-slice | bytes 12 | tf_op jit(solution)/shard_map/dynamic_slice | solution.py:195
  33.4 1.9 %collective-permute-start.4 = (bf16[64,2048]{1,0:T(8,128)(2,1)S(1)}, bf16[64,2048]{1,0:T(8,128)(2,1)S(1)}, u32[]{:S(2)}, u32[]{:S(2)}) collective-permute-start(bf16[64,2048]{1,0:T(8,128)(2,1)S(1)} %collective-permute-done.2.refs_3_), channel_id=1, source_target_pairs={{0,4},{4,8},{8,12},{12,14},{14,10},{10,6},{6,2},{2,0},{1,5},{5,9},... | collective-permute-start | bytes 786440 | tf_op jit(solution)/shard_map/ppermute | solution.py:201
  35.3 0.7 %collective-permute-start.5 = (bf16[64,2048]{1,0:T(8,128)(2,1)S(1)}, bf16[64,2048]{1,0:T(8,128)(2,1)S(1)}, u32[]{:S(2)}, u32[]{:S(2)}) collective-permute-start(bf16[64,2048]{1,0:T(8,128)(2,1)S(1)} %collective-permute-done.3.refs_4_), channel_id=1, source_target_pairs={{4,0},{8,4},{12,8},{14,12},{10,14},{6,10},{2,6},{0,2},{5,1},{9,5},... | collective-permute-start | bytes 786440 | tf_op jit(solution)/shard_map/ppermute | solution.py:202
  36.0 0.7 %compare_select_fusion = s32[8]{0:T(128)S(1)} fusion(s32[8]{0:T(128)S(1)} %copy-done.10, s32[]{:T(128)} %bitcast), kind=kLoop, calls=%fused_computation.4 | loop fusion | flops 120 | bytes 68 | tf_op jit(solution)/shard_map/select_n | solution.py:210
  36.7 1.2 %gather_fusion = s32[8]{0:T(128)} fusion(s32[8]{0:T(128)S(1)} %copy-done, s32[1024]{0:T(1024)S(1)} %pad_clamp_fusion), kind=kCustom, calls=%fused_computation | custom fusion | bytes 96 | tf_op jit(solution)/shard_map/gather | solution.py:210
  37.9 3.6 %collective-permute-done.4.refs_5_ = bf16[64,2048]{1,0:T(8,128)(2,1)S(1)} collective-permute-done((bf16[64,2048]{1,0:T(8,128)(2,1)S(1)}, bf16[64,2048]{1,0:T(8,128)(2,1)S(1)}, u32[]{:S(2)}, u32[]{:S(2)}) %collective-permute-start.4) | collective-permute-done | bytes 262176 | tf_op jit(solution)/shard_map/ppermute | solution.py:201
  41.5 1.6 %collective-permute-start.6 = (bf16[32,2048]{1,0:T(8,128)(2,1)S(1)}, bf16[32,2048]{1,0:T(8,128)(2,1)S(1)}, u32[]{:S(2)}, u32[]{:S(2)}) collective-permute-start(bf16[32,2048]{1,0:T(8,128)(2,1)S(1)} %slice.10), channel_id=1, source_target_pairs={{0,4},{4,8},{8,12},{12,14},{14,10},{10,6},{6,2},{2,0},{1,5},{5,9},... | collective-permute-start | bytes 393224 | tf_op jit(solution)/shard_map/ppermute | solution.py:207
  43.1 0.4 collective-permute-done.5.refs_6_
  43.5 1.0 %collective-permute-start.7 = (bf16[32,2048]{1,0:T(8,128)(2,1)S(1)}, bf16[32,2048]{1,0:T(8,128)(2,1)S(1)}, u32[]{:S(2)}, u32[]{:S(2)}) collective-permute-start(bf16[32,2048]{1,0:T(8,128)(2,1)S(1)} %slice.11), channel_id=1, source_target_pairs={{4,0},{8,4},{12,8},{14,12},{10,14},{6,10},{2,6},{0,2},{5,1},{9,5},... | collective-permute-start | bytes 393224 | tf_op jit(solution)/shard_map/ppermute | solution.py:207
  44.6 2.3 %all-gather = bf16[16,32,512]{2,1,0:T(8,128)(2,1)} all-gather(bf16[8,32,512]{2,1,0:T(8,128)(2,1)S(1)} %all-to-all-done.1), channel_id=2, replica_groups=mesh['group'=2,'seq'=8,'res'=2] {'res'}, dimensions={0}, use_global_device_ids=true | all-gather | bytes 786432 | tf_op jit(solution)/shard_map/all_gather | solution.py:216
  46.9 0.5 collective-permute-done.6.refs_7_
  47.4 1.2 %collective-permute-done.7.refs_8_ = bf16[32,2048]{1,0:T(8,128)(2,1)S(1)} collective-permute-done((bf16[32,2048]{1,0:T(8,128)(2,1)S(1)}, bf16[32,2048]{1,0:T(8,128)(2,1)S(1)}, u32[]{:S(2)}, u32[]{:S(2)}) %collective-permute-start.7) | collective-permute-done | bytes 131104 | tf_op jit(solution)/shard_map/ppermute | solution.py:207
  48.7 0.6 %copy-done.9 = bf16[32,2048]{1,0:T(8,128)(2,1)} copy-done((bf16[32,2048]{1,0:T(8,128)(2,1)}, bf16[32,2048]{1,0:T(8,128)(2,1)S(1)}, u32[]{:S(2)}) %copy-start.9) | copy-done | bytes 131096
  49.3 6.6 %pair.1 = bf16[16,64,128]{2,1,0:T(8,128)(2,1)} custom-call(s32[8]{0:T(128)} %gather_fusion, bf16[2,8,32,512]{3,2,1,0:T(8,128)(2,1)} %bitcast.19, bf16[4096,512]{1,0:T(8,128)(2,1)} %bitcast.17, f32[1,128]{1,0:T(1,128)} %bitcast.28, bf16[64,2048]{1,0:T(8,128)(2,1)} %get-tuple-element.8.refs_0_, bf16[64,2048]{1,0:T(8,128)(2,1)} %copy-done.4, ...), custom_call_target="tpu_custom_call" | custom-call | tf_op jit(solution)/shard_map/pair/pallas_call | solution.py:167
  (33 shorter events, 0.1 us)
Async XLA Ops:
  0.0 24.2 %copy-start.3 = (bf16[1024,128]{1,0:T(8,128)(2,1)S(1)}, bf16[1024,128]{1,0:T(8,128)(2,1)}, u32[]{:S(2)}) copy-start(bf16[1024,128]{1,0:T(8,128)(2,1)} %param.19) | copy-start | bytes 786436
  6.8 15.2 %collective-permute-start = (bf16[64,2048]{1,0:T(8,128)(2,1)}, bf16[64,2048]{1,0:T(8,128)(2,1)S(1)}, u32[]{:S(2)}, u32[]{:S(2)}) collective-permute-start(bf16[64,2048]{1,0:T(8,128)(2,1)} %get-tuple-element.8.refs_0_), channel_id=1, source_target_pairs={{0,4},{4,8},{8,12},{12,14},{14,10},{10,6},{6,2},{2,0},{1,5},{5,9},... | collective-permute-start | bytes 786440 | tf_op jit(solution)/shard_map/ppermute | solution.py:201
  9.9 14.2 %collective-permute-start.1 = (bf16[64,2048]{1,0:T(8,128)(2,1)}, bf16[64,2048]{1,0:T(8,128)(2,1)S(1)}, u32[]{:S(2)}, u32[]{:S(2)}) collective-permute-start(bf16[64,2048]{1,0:T(8,128)(2,1)} %get-tuple-element.8.refs_0_), channel_id=1, source_target_pairs={{4,0},{8,4},{12,8},{14,12},{10,14},{6,10},{2,6},{0,2},{5,1},{9,5},... | collective-permute-start | bytes 786440 | tf_op jit(solution)/shard_map/ppermute | solution.py:202
  15.7 28.9 %all-to-all-start.1 = ((bf16[8,32,512]{2,1,0:T(8,128)(2,1)}), bf16[8,32,512]{2,1,0:T(8,128)(2,1)S(1)}, u32[]{:S(2)}, u32[]{:S(2)}) async-start(bf16[8,32,512]{2,1,0:T(8,128)(2,1)} %bitcast.8), calls=%async_computation.1 | async-start | bytes 524288 | tf_op jit(solution)/shard_map/all_to_all | solution.py:215
  22.0 10.7 %copy-start.4 = (bf16[64,2048]{1,0:T(8,128)(2,1)}, bf16[64,2048]{1,0:T(8,128)(2,1)S(1)}, u32[]{:S(2)}) copy-start(bf16[64,2048]{1,0:T(8,128)(2,1)S(1)} %collective-permute-done.refs_1_) | copy-start | bytes 786436
  22.0 11.4 %collective-permute-start.2 = (bf16[64,2048]{1,0:T(8,128)(2,1)S(1)}, bf16[64,2048]{1,0:T(8,128)(2,1)S(1)}, u32[]{:S(2)}, u32[]{:S(2)}) collective-permute-start(bf16[64,2048]{1,0:T(8,128)(2,1)S(1)} %collective-permute-done.refs_1_), channel_id=1, source_target_pairs={{0,4},{4,8},{8,12},{12,14},{14,10},{10,6},{6,2},{2,0},{1,5},{5,9},... | collective-permute-start | bytes 786440 | tf_op jit(solution)/shard_map/ppermute | solution.py:201
  24.1 8.6 %copy-start.5 = (bf16[64,2048]{1,0:T(8,128)(2,1)}, bf16[64,2048]{1,0:T(8,128)(2,1)S(1)}, u32[]{:S(2)}) copy-start(bf16[64,2048]{1,0:T(8,128)(2,1)S(1)} %collective-permute-done.1.refs_2_) | copy-start | bytes 786436
  24.1 11.2 %collective-permute-start.3 = (bf16[64,2048]{1,0:T(8,128)(2,1)S(1)}, bf16[64,2048]{1,0:T(8,128)(2,1)S(1)}, u32[]{:S(2)}, u32[]{:S(2)}) collective-permute-start(bf16[64,2048]{1,0:T(8,128)(2,1)S(1)} %collective-permute-done.1.refs_2_), channel_id=1, source_target_pairs={{4,0},{8,4},{12,8},{14,12},{10,14},{6,10},{2,6},{0,2},{5,1},{9,5},... | collective-permute-start | bytes 786440 | tf_op jit(solution)/shard_map/ppermute | solution.py:202
  27.8 4.9 %copy-start.11 = (s32[8]{0:T(128)S(1)}, s32[8]{0:T(128)}, u32[]{:S(2)}) copy-start(s32[8]{0:T(128)} %constant.32.clone) | copy-start | bytes 100
  27.8 8.2 %copy-start.10 = (s32[8]{0:T(128)S(1)}, s32[8]{0:T(128)}, u32[]{:S(2)}) copy-start(s32[8]{0:T(128)} %constant.34.clone) | copy-start | bytes 100
  27.8 9.0 %copy-start = (s32[8]{0:T(128)S(1)}, s32[8]{0:T(128)}, u32[]{:S(2)}) copy-start(s32[8]{0:T(128)} %constant.33.clone) | copy-start | bytes 100
  33.4 15.3 %copy-start.6 = (bf16[64,2048]{1,0:T(8,128)(2,1)}, bf16[64,2048]{1,0:T(8,128)(2,1)S(1)}, u32[]{:S(2)}) copy-start(bf16[64,2048]{1,0:T(8,128)(2,1)S(1)} %collective-permute-done.2.refs_3_) | copy-start | bytes 786436
  33.4 8.2 %collective-permute-start.4 = (bf16[64,2048]{1,0:T(8,128)(2,1)S(1)}, bf16[64,2048]{1,0:T(8,128)(2,1)S(1)}, u32[]{:S(2)}, u32[]{:S(2)}) collective-permute-start(bf16[64,2048]{1,0:T(8,128)(2,1)S(1)} %collective-permute-done.2.refs_3_), channel_id=1, source_target_pairs={{0,4},{4,8},{8,12},{12,14},{14,10},{10,6},{6,2},{2,0},{1,5},{5,9},... | collective-permute-start | bytes 786440 | tf_op jit(solution)/shard_map/ppermute | solution.py:201
  35.3 13.3 %copy-start.7 = (bf16[64,2048]{1,0:T(8,128)(2,1)}, bf16[64,2048]{1,0:T(8,128)(2,1)S(1)}, u32[]{:S(2)}) copy-start(bf16[64,2048]{1,0:T(8,128)(2,1)S(1)} %collective-permute-done.3.refs_4_) | copy-start | bytes 786436
  35.3 8.2 %collective-permute-start.5 = (bf16[64,2048]{1,0:T(8,128)(2,1)S(1)}, bf16[64,2048]{1,0:T(8,128)(2,1)S(1)}, u32[]{:S(2)}, u32[]{:S(2)}) collective-permute-start(bf16[64,2048]{1,0:T(8,128)(2,1)S(1)} %collective-permute-done.3.refs_4_), channel_id=1, source_target_pairs={{4,0},{8,4},{12,8},{14,12},{10,14},{6,10},{2,6},{0,2},{5,1},{9,5},... | collective-permute-start | bytes 786440 | tf_op jit(solution)/shard_map/ppermute | solution.py:202
  41.5 7.1 %copy-start.1 = (bf16[64,2048]{1,0:T(8,128)(2,1)}, bf16[64,2048]{1,0:T(8,128)(2,1)S(1)}, u32[]{:S(2)}) copy-start(bf16[64,2048]{1,0:T(8,128)(2,1)S(1)} %collective-permute-done.4.refs_5_) | copy-start | bytes 786436
  41.5 5.9 %collective-permute-start.6 = (bf16[32,2048]{1,0:T(8,128)(2,1)S(1)}, bf16[32,2048]{1,0:T(8,128)(2,1)S(1)}, u32[]{:S(2)}, u32[]{:S(2)}) collective-permute-start(bf16[32,2048]{1,0:T(8,128)(2,1)S(1)} %slice.10), channel_id=1, source_target_pairs={{0,4},{4,8},{8,12},{12,14},{14,10},{10,6},{6,2},{2,0},{1,5},{5,9},... | collective-permute-start | bytes 393224 | tf_op jit(solution)/shard_map/ppermute | solution.py:207
  43.5 5.1 %copy-start.2 = (bf16[64,2048]{1,0:T(8,128)(2,1)}, bf16[64,2048]{1,0:T(8,128)(2,1)S(1)}, u32[]{:S(2)}) copy-start(bf16[64,2048]{1,0:T(8,128)(2,1)S(1)} %collective-permute-done.5.refs_6_) | copy-start | bytes 786436
  43.5 5.1 %collective-permute-start.7 = (bf16[32,2048]{1,0:T(8,128)(2,1)S(1)}, bf16[32,2048]{1,0:T(8,128)(2,1)S(1)}, u32[]{:S(2)}, u32[]{:S(2)}) collective-permute-start(bf16[32,2048]{1,0:T(8,128)(2,1)S(1)} %slice.11), channel_id=1, source_target_pairs={{4,0},{8,4},{12,8},{14,12},{10,14},{6,10},{2,6},{0,2},{5,1},{9,5},... | collective-permute-start | bytes 393224 | tf_op jit(solution)/shard_map/ppermute | solution.py:207
  47.4 1.3 %copy-start.8 = (bf16[32,2048]{1,0:T(8,128)(2,1)}, bf16[32,2048]{1,0:T(8,128)(2,1)S(1)}, u32[]{:S(2)}) copy-start(bf16[32,2048]{1,0:T(8,128)(2,1)S(1)} %collective-permute-done.6.refs_7_) | copy-start | bytes 393220
  48.6 0.6 %copy-start.9 = (bf16[32,2048]{1,0:T(8,128)(2,1)}, bf16[32,2048]{1,0:T(8,128)(2,1)S(1)}, u32[]{:S(2)}) copy-start(bf16[32,2048]{1,0:T(8,128)(2,1)S(1)} %collective-permute-done.7.refs_8_) | copy-start | bytes 393220
